TPU v7x, 256 devices: a whole 4x4x8 slice. The times are simulated.
256 devices in a mesh: dp: 32 (over z, y_lo, core), mp: 8 (over y_hi, x).
Axes of the slice: x: 4, y: 4 (y_hi: 2, y_lo: 2; y = y_hi * 2 + y_lo), z: 8, core: 2. Of those that a mesh axis runs over, the one named last changes fastest.
Arguments:
- upper_first: bfloat16 [8192, 4096], P('dp'), may hold values from -6 to 6
- upper_second: bfloat16 [8192, 4096], P('dp'), may hold values from -24 to 24
- grad_first: bfloat16 [8192, 4096], P('dp'), may hold values from -6 to 6
- grad_second: bfloat16 [8192, 4096], P('dp'), may hold values from -6 to 6
- norm_gain: bfloat16 [4096], replicated, may hold values from 0.25 to 1.75
- up_weight: bfloat16 [4096, 11264], P('dp', 'mp'), may hold values from -0.09375 to 0.09375
- down_weight: bfloat16 [4096, 11264], P('dp', 'mp'), may hold values from -0.0546875 to 0.0546875
- adapter_down: bfloat16 [4096, 64], replicated, may hold values from -0.09375 to 0.09375
- adapter_up: bfloat16 [64, 4096], replicated, may hold values from -0.75 to 0.75
Outputs:
- lower_first: bfloat16 [8192, 4096], P('dp', 'mp')
- lower_second: bfloat16 [8192, 4096], P('dp', 'mp')
- input_grad_first: bfloat16 [8192, 4096], P('dp', 'mp')
- input_grad_second: bfloat16 [8192, 4096], P('dp')
- adapter_down_grad: float32 [4096, 64], P('mp')
- adapter_up_grad: float32 [64, 4096], P(None, 'mp')
All inputs are finite; a program needn't handle non-finite values.
Results may differ from a plain program's by a relative error of at most 0.009.
Values may be sent and summed in bfloat16 or wider, within the bound.
A program may use at most 128 MiB of HBM per device.

v0:
```python
import math

import jax
import jax.numpy as jnp
from jax import lax
from jax.sharding import PartitionSpec as P

coupling = 0.5


def silu_slope(argument):
    sigmoid_value = jax.nn.sigmoid(argument)
    return sigmoid_value * (1.0 + argument * (1.0 - sigmoid_value))


def on_device(
    upper_first,
    upper_second,
    grad_first,
    grad_second,
    norm_gain,
    up_weight,
    down_weight,
    adapter_down,
    adapter_up,
):
    groups = lax.axis_size("mp")
    mp_rank = lax.axis_index("mp")
    model_width = upper_first.shape[1]
    share_width = model_width // groups
    offset = mp_rank * share_width
    tokens_all = upper_first.shape[0] * lax.axis_size("dp")
    grad_scale = 1.0 / math.sqrt(tokens_all)
    up_full = lax.all_gather(up_weight, "dp", axis=0, tiled=True)
    pre_adapter = jnp.dot(upper_first, adapter_down, preferred_element_type=jnp.float32)
    squashed = jax.nn.silu(pre_adapter).astype(jnp.bfloat16)
    adapted = jnp.dot(squashed, adapter_up, preferred_element_type=jnp.float32)
    lower_full = (upper_second.astype(jnp.float32) - adapted).astype(jnp.bfloat16)
    lower_value = lower_full.astype(jnp.float32)
    inverse_rms = lax.rsqrt(jnp.mean(lower_value * lower_value, axis=1, keepdims=True) + 1e-05)
    gain_full = norm_gain.astype(jnp.float32)
    normed = (lower_value * inverse_rms * gain_full).astype(jnp.bfloat16)
    hidden_pre = jnp.dot(normed, up_full, preferred_element_type=jnp.float32)
    activated = jax.nn.silu(hidden_pre).astype(jnp.bfloat16)
    down_full = lax.all_gather(down_weight, "dp", axis=0, tiled=True)
    partial_out = lax.dot_general(
        activated, down_full, (((1,), (1,)), ((), ())), preferred_element_type=jnp.float32
    )
    frozen_share = lax.psum_scatter(
        partial_out.astype(jnp.bfloat16), "mp", scatter_dimension=1, tiled=True
    ).astype(jnp.float32)
    upper_slice = lax.dynamic_slice_in_dim(upper_first, offset, share_width, 1)
    lower_first = ((upper_slice.astype(jnp.float32) - frozen_share) / coupling).astype(jnp.bfloat16)
    adapter_slope = jnp.einsum(
        "td,rd->tr", grad_second, adapter_up, preferred_element_type=jnp.float32
    )
    adapter_pre_grad = (adapter_slope * silu_slope(pre_adapter)).astype(jnp.bfloat16)
    back_adapter = jnp.einsum(
        "tr,dr->td", adapter_pre_grad, adapter_down, preferred_element_type=jnp.float32
    )
    carried = (grad_first.astype(jnp.float32) + back_adapter).astype(jnp.bfloat16)
    carried_slice = lax.dynamic_slice_in_dim(carried, offset, share_width, 1)
    input_grad_first = (coupling * carried_slice.astype(jnp.float32)).astype(jnp.bfloat16)
    down_grad_part = (
        jnp.einsum("td,tr->dr", upper_slice, adapter_pre_grad, preferred_element_type=jnp.float32)
        * grad_scale
    )
    second_slice = lax.dynamic_slice_in_dim(grad_second, offset, share_width, 1)
    up_grad_part = (
        jnp.einsum("tr,td->rd", squashed, second_slice, preferred_element_type=jnp.float32)
        * grad_scale
    )
    adapter_down_grad, adapter_up_grad = lax.psum((down_grad_part, up_grad_part), "dp")
    act_grad = jnp.dot(carried, down_full, preferred_element_type=jnp.float32)
    pre_grad = (act_grad * silu_slope(hidden_pre)).astype(jnp.bfloat16)
    normed_part = lax.dot_general(
        pre_grad, up_full, (((1,), (1,)), ((), ())), preferred_element_type=jnp.float32
    )
    stat_part = jnp.sum(hidden_pre * pre_grad.astype(jnp.float32), axis=1)
    normed_grad, curvature = lax.psum((normed_part, stat_part), "mp")
    correction = lower_value * inverse_rms * inverse_rms * curvature[:, None] / model_width
    input_grad_second = (
        grad_second.astype(jnp.float32) + inverse_rms * gain_full * normed_grad - correction
    ).astype(jnp.bfloat16)
    lower_second = lax.dynamic_slice_in_dim(lower_full, offset, share_width, 1)
    return (
        lower_first,
        lower_second,
        input_grad_first,
        input_grad_second,
        adapter_down_grad,
        adapter_up_grad,
    )


def solution(mesh):
    return jax.shard_map(
        on_device,
        mesh=mesh,
        in_specs=(
            P("dp", None),
            P("dp", None),
            P("dp", None),
            P("dp", None),
            P(),
            P("dp", "mp"),
            P("dp", "mp"),
            P(),
            P(),
        ),
        out_specs=(
            P("dp", "mp"),
            P("dp", "mp"),
            P("dp", "mp"),
            P("dp", None),
            P("mp", None),
            P(None, "mp"),
        ),
        check_vma=False,
    )
```

profile of v0, /device:TPU:1, one launch (start us, length us, event | category | flops | bytes accessed | tf_op | source)
XLA Modules:
  0.0 618.4 jit_solution(9565982590470995360)
XLA Ops:
  8.7 0.8 convert_element_type.65
  9.6 2.4 fusion.22
  12.0 2.2 fusion.9
  14.3 0.8 fusion.15
  15.0 0.8 copy-done.2
  15.9 2.1 fusion.1
  18.0 72.4 %all-gather.3.cloned.1.call-done = bf16[4096,1408]{1,0:T(8,128)(2,1)} async-done(((bf16[128,1408]{1,0:T(8,128)(2,1)}), bf16[4096,1408]{1,0:T(8,128)(2,1)}) %all-gather.3.cloned.1.call-update) | async-done | bytes 11534352 | tf_op jit(solution)/shard_map/all_gather | solution.py:34
  90.4 9.6 %fusion.11 = f32[256,1408]{1,0:T(8,128)} fusion(bf16[4096,1408]{1,0:T(8,128)(2,1)} %all-gather.3.cloned.1.call-done, bf16[256,4096]{1,0:T(8,128)(2,1)} %get-tuple-element.9, f32[4096]{0:T(1024)S(1)} %convert_element_type.65, f32[256]{0:T(256)S(1)} %add_rsqrt_fusion), kind=kOutput, calls=%fused_computation.17 | convolution fusion | flops 2956984320 | bytes 15090688 | tf_op jit(solution)/shard_map/dot_general | solution.py:43
  99.9 67.4 %all-gather.5.cloned.1.call-done = bf16[4096,1408]{1,0:T(8,128)(2,1)} async-done(((bf16[128,1408]{1,0:T(8,128)(2,1)}), bf16[4096,1408]{1,0:T(8,128)(2,1)}) %all-gather.5.cloned.1.call-update) | async-done | bytes 11534352 | tf_op jit(solution)/shard_map/all_gather | solution.py:45
  167.3 9.0 %multiply_reduce_fusion = (f32[256]{0:T(256)S(1)}, bf16[256,1408]{1,0:T(8,128)(2,1)S(1)}) fusion(f32[256,1408]{1,0:T(8,128)} %fusion.11, bf16[256,4096]{1,0:T(8,128)(2,1)} %fusion.1, bf16[4096,1408]{1,0:T(8,128)(2,1)} %all-gather.5.cloned.1.call-done), kind=kOutput, calls=%fused_computation.20 | convolution fusion | flops 2957115136 | bytes 15795200 | tf_op jit(solution)/shard_map/dot_general | solution.py:74
  176.3 5.0 fusion.23
  181.6 9.6 %convolution_convert_fusion = bf16[256,4096]{1,0:T(8,128)(2,1)} fusion(bf16[4096,1408]{1,0:T(8,128)(2,1)} %all-gather.5.cloned.1.call-done, f32[256,1408]{1,0:T(8,128)} %fusion.11), kind=kOutput, calls=%fused_computation.6 | convolution fusion | flops 2955640832 | bytes 15073280 | tf_op jit(solution)/shard_map/dot_general | solution.py:46
  191.2 1.8 convolution_multiply_fusion.1
  193.0 0.8 convolution_multiply_fusion.2
  193.9 1.7 constant_dynamic-slice_fusion
  195.6 1.7 multiply_convert_fusion.2
  197.2 21.3 %psum.29 = f32[256]{0:T(256)S(1)} all-reduce(f32[256]{0:T(256)S(1)} %get-tuple-element.10), channel_id=1, replica_groups=mesh['dp'=32,'mp'=8] {'mp'}, use_global_device_ids=true, to_apply=%region_4.5 | all-reduce | flops 256 | bytes 2048 | tf_op jit(solution)/shard_map/psum | solution.py:80
  218.5 76.4 %all-reduce.4.cloned.1.call-done = f32[256,4096]{1,0:T(8,128)} async-done(((f32[256,4096]{1,0:T(8,128)}), f32[256,4096]{1,0:T(8,128)}) %all-reduce.4.cloned.1.call-update) | async-done | bytes 4194320 | tf_op jit(solution)/shard_map/psum | solution.py:80
  294.9 5.8 fusion.8
  300.7 77.4 %reduce-scatter.2.cloned.1.call-done = bf16[256,512]{1,0:T(8,128)(2,1)} async-done(((bf16[256,4096]{1,0:T(8,128)(2,1)}), bf16[256,512]{1,0:T(8,128)(2,1)}) %reduce-scatter.2.cloned.1.call-update) | async-done | bytes 262160 | tf_op jit(solution)/shard_map/reduce_scatter | solution.py:49
  378.1 1.8 multiply_convert_fusion.3
  379.9 228.8 %all-reduce.6.cloned.1.call-done = (f32[512,64]{0,1:T(8,128)}, f32[64,512]{1,0:T(8,128)}) async-done(((f32[512,64]{0,1:T(8,128)}, f32[64,512]{1,0:T(8,128)}), (f32[512,64]{0,1:T(8,128)}, f32[64,512]{1,0:T(8,128)})) %all-reduce.6.cloned.1.call-update) | async-done | bytes 262160 | tf_op jit(solution)/shard_map/psum | solution.py:73
  608.8 1.6 copy.18
  610.4 1.6 copy.19
  (22 shorter events, 1.9 us)
Async XLA Ops:
  7.2 4.8 copy-start
  7.2 83.2 %all-gather.3.cloned.1.call-start = ((), (), s32[]{:S(2)}) async-start(), calls=%async_computation.1 | async-start | bytes 11894784 | tf_op jit(solution)/shard_map/all_gather | solution.py:34
  7.9 159.4 %all-gather.5.cloned.1.call-start = ((), (), s32[]{:S(2)}) async-start(), calls=%async_computation.2 | async-start | bytes 11894784 | tf_op jit(solution)/shard_map/all_gather | solution.py:45
  8.7 286.3 %all-reduce.4.cloned.1.call-start = ((), (), s32[]{:S(2)}) async-start(), calls=%async_computation.4 | async-start | bytes 8388608 | tf_op jit(solution)/shard_map/psum | solution.py:80
  8.7 3.3 copy-start.5
  12.0 2.2 copy-start.1
  14.3 1.6 copy-start.2
  14.3 1.7 copy-start.3
  167.3 9.0 %copy-start.4 = (bf16[4096,1408]{1,0:T(8,128)(2,1)S(1)}, bf16[4096,1408]{1,0:T(8,128)(2,1)}, u32[]{:S(2)}) copy-start(bf16[4096,1408]{1,0:T(8,128)(2,1)} %all-gather.3.cloned.1.call-done) | copy-start | bytes 34603012
  181.4 196.8 %reduce-scatter.2.cloned.1.call-start = ((), (), s32[]{:S(2)}) async-start(), calls=%async_computation.3 | async-start | bytes 2359296 | tf_op jit(solution)/shard_map/reduce_scatter | solution.py:49
  191.2 417.6 %all-reduce.6.cloned.1.call-start = ((), (), s32[]{:S(2)}) async-start(), calls=%async_computation.5 | async-start | bytes 524288 | tf_op jit(solution)/shard_map/psum | solution.py:73
Sparse Core Ops, SparseCore 0:
  9.8 80.4 all-gather.2
  92.2 75.0 all-gather.4
  181.5 113.4 all-reduce.3
  298.9 79.2 reduce-scatter.1
  381.2 227.5 all-reduce.5
where the time goes:
time: 619 us; the launch traced here: 618 us
  waiting for transfers between devices  524 us (85%)
  matrix products  43.3 us (7%)
  blocking collectives  21.3 us (3%)
  between operations  13.9 us (2%)
  other arithmetic  10.2 us (2%)
    psum x1, waiting for transfers between devices, on_device(): lax.psum((down_grad_part, up_grad_part), 'dp')  229 us
    reduce_scatter x1, waiting for transfers between devices, on_device(): lax.psum_scatter(partial_out.astype(jnp.bfloat16), 'mp', scatter_dimensio...  77.4 us
    psum x1, waiting for transfers between devices, on_device(): normed_grad, curvature = lax.psum((normed_part, stat_part), 'mp')  76.4 us
    all_gather x1, waiting for transfers between devices, on_device(): up_full = lax.all_gather(up_weight, 'dp', axis=0, tiled=True)  72.4 us
    all_gather x1, waiting for transfers between devices, on_device(): down_full = lax.all_gather(down_weight, 'dp', axis=0, tiled=True)  67.4 us
    psum x1, blocking collectives, on_device(): normed_grad, curvature = lax.psum((normed_part, stat_part), 'mp')  21.3 us
  transfers between devices with their start and end apart: 5, of which 5 were waited for; matrix products, arithmetic and copies ran while one was open for 7% of the time, Pallas kernels for 0%

commit v1 on v0

v1 whole, which is shorter than its diff:
```python
import functools
import math

import jax
import jax.numpy as jnp
from jax import lax
from jax.experimental import pallas as pl
from jax.experimental.pallas import tpu as pltpu
from jax.sharding import PartitionSpec as P

MESH = pl.DeviceIdType.MESH
D = 4096
H = 1408
T = 256
R = 64
NZ = 8
NM = 8
UNIT = 64
CARRY = 3
GROUP = 256
LAYER = 512
CHUNKS = D // GROUP
HCUTS = ((0, 512), (512, 512), (1024, 384))
SHARE = T // NM
F32 = jnp.float32
BF16 = jnp.bfloat16
GRAD_SCALE = 1.0 / math.sqrt(8192.0)


def dot(a, b):
    return jnp.dot(a, b, preferred_element_type=F32)


def dot_nt(a, b):
    return lax.dot_general(a, b, (((1,), (1,)), ((), ())), preferred_element_type=F32)


def sigmoid(v):
    return 1.0 / (1.0 + jnp.exp(-v))


def wait_bytes(ref, sem):
    pltpu.make_async_copy(ref, ref, sem).wait()


def kernel(
    uf_hbm, us_hbm, gf_hbm, gs_hbm, gain_ref, upw, dnw, adt_hbm, au_hbm,
    o_lf, o_ls, o_igf, o_igs, o_dg, o_ug,
    uf, us, gf, gs, norm, adt, au,
    up, dn, hp, ag, slope, act, pg,
    fs, fr, ns, nr, outc,
    pre, sl, ssq, invb, curv, stat, sr,
    grad, gr1, gr2, gr3, gfin,
    in_sem, ad_sem, init_sem, isend, zrecv, zsend, yrecv, ysend, srecv, ssend,
    fsend, frecv, nsend, nrecv, tsend, trecv, gsend, grecv, osend, orecv, osem,
):
    dp = lax.axis_index("dp")
    m = lax.axis_index("mp")
    c = lax.rem(dp, 2)
    y = lax.rem(dp // 2, 2)
    z = dp // 4
    home = jnp.where(y == c, 1, 0)

    def dev(z_, y_, c_, m_):
        return ((z_ * 2 + y_) * 2 + c_, m_)

    sib = dev(z, y, 1 - c, m)
    ypal = dev(z, 1 - y, c, m)
    step_z = jnp.where(c == 0, 1, NZ - 1)
    znext = dev(lax.rem(z + step_z, NZ), y, c, m)
    zshift = [lax.rem(z + k, NZ) for k in range(NZ)]
    mshift = [lax.rem(m + k, NM) for k in range(NM)]
    zdev = [dev(zshift[k], y, c, m) for k in range(NZ)]
    mdev = [dev(z, y, c, mshift[k]) for k in range(NM)]

    def send(src, dst, ssem, rsem, to):
        pltpu.make_async_remote_copy(
            src_ref=src, dst_ref=dst, send_sem=ssem, recv_sem=rsem, device_id=to, device_id_type=MESH
        ).start()

    barrier = pltpu.get_barrier_semaphore()
    partners = [zdev[k] for k in range(1, NZ)] + [dev(z, 1 - y, 0, m), dev(z, 1 - y, 1, m), sib]
    partners += [mdev[k] for k in range(1, NM)]
    for p in partners:
        pl.semaphore_signal(barrier, inc=1, device_id=p, device_id_type=MESH)
    pl.semaphore_wait(barrier, len(partners))

    weights = ((upw, up), (dnw, dn))
    first = z * LAYER + y * GROUP + c * 128
    for w, (src, dst) in enumerate(weights):
        for h in range(2):
            rows = pl.ds(pl.multiple_of(first + h * UNIT, UNIT), UNIT)
            piece = src.at[pl.ds(h * UNIT, UNIT)]
            send(piece, dst.at[rows], isend.at[w, 0], init_sem.at[w, 2 * c + h], dev(z, 1 - y, y, m))

            @pl.when(home == 1)
            def _():
                pltpu.make_async_copy(piece, dst.at[rows], init_sem.at[w, 2 * c + h]).start()

            @pl.when(home == 0)
            def _():
                send(piece, dst.at[rows], isend.at[w, 1], init_sem.at[w, 2 * c + h], sib)

    ins = ((uf_hbm, uf), (gs_hbm, gs), (us_hbm, us), (gf_hbm, gf))
    for src, dst in ((adt_hbm, adt), (au_hbm, au)):
        for k in range(CHUNKS):
            pltpu.make_async_copy(src.at[:, pl.ds(k * GROUP, GROUP)], dst.at[k], ad_sem).start()
    for i, (src, dst) in enumerate(ins):
        for k in range(CHUNKS):
            pltpu.make_async_copy(src.at[:, pl.ds(k * GROUP, GROUP)], dst.at[k], in_sem.at[i]).start()

    def own_layer(s):
        return lax.rem(jnp.where(c == 0, z + NZ - s, z + s), NZ)

    def sib_layer(s):
        return lax.rem(jnp.where(c == 0, z + s, z + NZ - s), NZ)

    def rows_at(layer, group, offset, count):
        return pl.ds(pl.multiple_of(layer * LAYER + group * GROUP + offset, UNIT), count)

    def poll(w, s):
        first_step = isinstance(s, int) and s == 0
        buf = weights[w][1]
        layer = own_layer(s)
        for j in range(CARRY):
            region = buf.at[rows_at(layer, c, UNIT * home + UNIT * j, UNIT)]
            wait_bytes(region, init_sem.at[w, j + home] if first_step else zrecv.at[w, s, j])

            @pl.when(s < NZ - 1)
            def _():
                send(region, region, zsend.at[w], zrecv.at[w, s + 1, j], znext)

        if not first_step:
            region = buf.at[rows_at(layer, c, 3 * UNIT * home, UNIT)]
            send(region, region, ysend.at[w], yrecv.at[w, s], ypal)

    def late(w, s):
        first_step = isinstance(s, int) and s == 0
        buf = weights[w][1]
        layer = own_layer(s)
        region = buf.at[rows_at(layer, c, 3 * UNIT * (1 - home), UNIT)]
        wait_bytes(region, init_sem.at[w, 3 * (1 - home)] if first_step else yrecv.at[w, s])
        region = buf.at[rows_at(layer, c, 0, GROUP)]
        send(region, region, ssend.at[w], srecv.at[w, s], sib)

    def ready(w, s):
        wait_bytes(weights[w][1].at[rows_at(sib_layer(s), 1 - c, 0, GROUP)], srecv.at[w, s])

    def product_step(w, s, left, acc):
        buf = weights[w][1]
        own, other = own_layer(s), sib_layer(s)
        own_rows, other_rows = rows_at(own, c, 0, GROUP), rows_at(other, 1 - c, 0, GROUP)
        a, b = left[own * 2 + c], left[other * 2 + 1 - c]
        for lo, n in HCUTS:
            acc[:, lo:lo + n] += dot(a, buf[own_rows, lo:lo + n]) + dot(b, buf[other_rows, lo:lo + n])

    def hidden_step(s):
        ready(0, s)
        product_step(0, s, norm, hp)

    def frozen_block(layer, group):
        k = layer * 2 + group
        fs[k] = dot_nt(act[...], dn[rows_at(layer, group, 0, GROUP), :]).astype(BF16)
        shift = lax.rem(layer + NM - m, NM)

        @pl.when(shift != 0)
        def _():
            send(fs.at[k], fr.at[shift - 1, group], fsend, frecv, (dp, layer))

    def down_step(s):
        ready(1, s)
        product_step(1, s, gf, ag)
        frozen_block(own_layer(s), c)
        frozen_block(sib_layer(s), 1 - c)

    def adapter_in():
        wait_bytes(adt, ad_sem)
        wait_bytes(au, ad_sem)
        wait_bytes(uf, in_sem.at[0])
        wait_bytes(gs, in_sem.at[1])
        pre[...] = jnp.zeros_like(pre)
        sl[...] = jnp.zeros_like(sl)

        def body(k, _):
            pre[...] += dot_nt(uf[k], adt[k])
            sl[...] += dot_nt(gs[k], au[k])
            return 0

        lax.fori_loop(0, CHUNKS, body, 0)
        v = pre[...]
        s = sigmoid(v)
        pre[...] = v * s
        sl[...] = sl[...] * (s * (1.0 + v * (1.0 - s)))
        wait_bytes(us, in_sem.at[2])
        wait_bytes(gf, in_sem.at[3])
        ssq[...] = jnp.zeros_like(ssq)

    def adapter_out(lo, hi):
        squashed = pre[...].astype(BF16)
        slope_in = sl[...].astype(BF16)

        def body(k, _):
            lower = (us[k].astype(F32) - dot(squashed, au[k])).astype(BF16)
            us[k] = lower
            value = lower.astype(F32)
            square = value * value
            ssq[...] += square[:, :128] + square[:, 128:]
            gf[k] = (gf[k].astype(F32) + dot(slope_in, adt[k])).astype(BF16)
            return 0

        lax.fori_loop(lo, hi, body, 0)

    def normalise():
        mean = jnp.sum(ssq[...], axis=1, keepdims=True) * (1.0 / D)
        invb[...] = jnp.broadcast_to(lax.rsqrt(mean + 1e-05), (T, 128))

        def body(k, _):
            scale = invb[...]
            both = jnp.concatenate([scale, scale], axis=1)
            norm[k] = (us[k].astype(F32) * both * gain_ref[k]).astype(BF16)
            return 0

        lax.fori_loop(0, CHUNKS, body, 0)
        hp[...] = jnp.zeros_like(hp)
        ag[...] = jnp.zeros_like(ag)

    def grads_1():
        both = jnp.concatenate([sl[...], pre[...]], axis=1)
        turned = both.T.astype(BF16)
        for half, (rows, right) in enumerate(((turned[:R], uf), (turned[R:], gs))):
            for q in range(2):
                part = dot(rows, right[2 * m + q])
                for yy in range(2):
                    for t in range(4):
                        lo = yy * 32 + t * 8
                        grad[half, yy, 2 * t + q] = part[lo:lo + 8]
        send(grad.at[1 - c], gr1, gsend.at[0], grecv.at[0], sib)

    def grads_2():
        wait_bytes(gr1, grecv.at[0])
        grad[c] = grad[c] + gr1[...]
        send(grad.at[c, 1 - y], gr2, gsend.at[1], grecv.at[1], ypal)

    def grads_3():
        wait_bytes(gr2, grecv.at[1])
        grad[c, y] = grad[c, y] + gr2[...]
        for k in range(1, NZ):
            send(grad.at[c, y, zshift[k]], gr3.at[k - 1], gsend.at[2], grecv.at[2], zdev[k])

    def grads_4():
        wait_bytes(gr3, grecv.at[2])
        total = grad[c, y, z]
        for k in range(NZ - 1):
            total = total + gr3[k]
        gfin[c, y, z] = total * GRAD_SCALE
        for k in range(1, NZ):
            send(gfin.at[c, y, z], gfin.at[c, y, z], gsend.at[3], grecv.at[3], zdev[k])

    def grads_5():
        wait_bytes(gr3, grecv.at[3])
        send(gfin.at[c, y], gfin.at[c, y], gsend.at[4], grecv.at[4], ypal)

    def grads_6():
        wait_bytes(gr2, grecv.at[4])
        send(gfin.at[c], gfin.at[c], gsend.at[5], grecv.at[5], sib)

    def grads_7():
        wait_bytes(gr1, grecv.at[5])
        for half, out in enumerate((o_dg, o_ug)):
            for yy in range(2):
                for t in range(4):
                    for q in range(2):
                        lo = yy * 32 + t * 8
                        out[lo:lo + 8, q * 256:q * 256 + 256] = gfin[half, yy, 2 * t + q]

    def activations():
        def body(i, _):
            rows = pl.ds(pl.multiple_of(i * 32, 32), 32)
            v = hp[rows, :]
            s = sigmoid(v)
            act[rows, :] = (v * s).astype(BF16)
            slope[rows, :] = s * (1.0 + v * (1.0 - s))
            return 0

        lax.fori_loop(0, 8, body, 0)

    def slices_out():
        for q in range(2):
            lo = q * 256
            o_ls[:, lo:lo + 256] = us[2 * m + q]
            o_igf[:, lo:lo + 256] = (0.5 * gf[2 * m + q].astype(F32)).astype(BF16)

    poll(0, 0)
    adapter_in()
    late(0, 0)
    poll(0, 1)
    adapter_out(0, CHUNKS // 2)
    late(0, 1)
    poll(0, 2)
    adapter_out(CHUNKS // 2, CHUNKS)
    late(0, 2)
    normalise()

    def up_body(s, _):
        poll(0, s)
        late(0, s - 1)

        @pl.when(s == 4)
        def _():
            grads_1()

        @pl.when(s == 5)
        def _():
            grads_2()

        @pl.when(s == 6)
        def _():
            grads_3()

        hidden_step(s - 3)
        return 0

    late_done = 3
    poll(0, 3)
    hidden_step(0)
    lax.fori_loop(late_done + 1, NZ, up_body, 0)
    poll(1, 0)
    hidden_step(5)
    late(0, 7)
    hidden_step(6)
    late(1, 0)
    poll(1, 1)
    hidden_step(7)
    activations()

    def down_body(s, _):
        poll(1, s)
        late(1, s - 1)

        @pl.when(s == 2)
        def _():
            grads_4()

        @pl.when(s == 3)
        def _():
            grads_5()

        @pl.when(s == 4)
        def _():
            grads_6()

        @pl.when(s == 5)
        def _():
            grads_7()
            slices_out()

        down_step(s - 2)
        return 0

    lax.fori_loop(2, NZ, down_body, 0)
    late(1, 7)
    down_step(6)
    down_step(7)

    def pre_grads(i, _):
        rows = pl.ds(pl.multiple_of(i * 32, 32), 32)
        g = (ag[rows, :] * slope[rows, :]).astype(BF16)
        pg[rows, :] = g
        part = jnp.sum(hp[rows, :] * g.astype(F32), axis=1, keepdims=True)
        stat[rows, :] = jnp.broadcast_to(part, (32, 128))
        return 0

    lax.fori_loop(0, 8, pre_grads, 0)
    mine = pl.ds(pl.multiple_of(m * SHARE, SHARE), SHARE)
    for k in range(1, NM):
        theirs = pl.ds(pl.multiple_of(mshift[k] * SHARE, SHARE), SHARE)
        send(stat.at[theirs], sr.at[k - 1], tsend, trecv, mdev[k])

    def normed_block(b, _):
        for q in range(2):
            rows = pl.ds(pl.multiple_of(b * LAYER + q * GROUP, GROUP), GROUP)
            ns[b, :, q * GROUP:q * GROUP + GROUP] = dot_nt(pg[...], up[rows, :]).astype(BF16)
        for k in range(1, NM):
            theirs = pl.ds(pl.multiple_of(mshift[k] * SHARE, SHARE), SHARE)
            send(ns.at[b, theirs], nr.at[b, k - 1], nsend, nrecv.at[b], mdev[k])
        return 0

    lax.fori_loop(0, NZ, normed_block, 0)

    wait_bytes(fr, frecv)
    for q in range(2):
        def rebuild(i, _):
            rows = pl.ds(pl.multiple_of(i * 32, 32), 32)
            total = fs[2 * m + q, rows, :].astype(F32)
            for k in range(NM - 1):
                total = total + fr[k, q, rows, :].astype(F32)
            o_lf[rows, q * GROUP:q * GROUP + GROUP] = (
                (uf[2 * m + q, rows, :].astype(F32) - total) * 2.0
            ).astype(BF16)
            return 0

        lax.fori_loop(0, 8, rebuild, 0)

    wait_bytes(sr, trecv)
    inv32 = invb[mine, :]
    total = stat[mine, :]
    for k in range(NM - 1):
        total = total + sr[k]
    curv[...] = inv32 * inv32 * total * (1.0 / D)

    def finish(b, _):
        wait_bytes(nr.at[b], nrecv.at[b])
        inv = invb[mine, :]
        inv = jnp.concatenate([inv, inv], axis=1)
        cv = jnp.concatenate([curv[...], curv[...]], axis=1)
        for q in range(2):
            lo = q * GROUP
            k2 = 2 * b + q
            normed_grad = ns[b, mine, lo:lo + GROUP].astype(F32)
            for k in range(NM - 1):
                normed_grad = normed_grad + nr[b, k, :, lo:lo + GROUP].astype(F32)
            outc[b, :, lo:lo + GROUP] = (
                gs[k2, mine, :].astype(F32)
                + inv * gain_ref[k2] * normed_grad
                - us[k2, mine, :].astype(F32) * cv
            ).astype(BF16)
        place = o_igs.at[mine, pl.ds(pl.multiple_of(b * LAYER, LAYER), LAYER)]
        for k in range(1, NM):
            send(outc.at[b], place, osend, orecv, mdev[k])
        pltpu.make_async_copy(outc.at[b], place, osem).start()
        return 0

    lax.fori_loop(0, NZ, finish, 0)

    seven = ns.at[:, pl.ds(0, T - SHARE)]
    for w in range(2):
        buf = weights[w][1]
        wait_bytes(buf.at[pl.ds(0, 2 * UNIT)], isend.at[w, 0])

        @pl.when(home == 0)
        def _():
            wait_bytes(buf.at[pl.ds(0, 2 * UNIT)], isend.at[w, 1])

        wait_bytes(buf.at[pl.ds(0, 7 * CARRY * UNIT)], zsend.at[w])
        wait_bytes(buf.at[pl.ds(0, 7 * UNIT)], ysend.at[w])
        wait_bytes(buf.at[pl.ds(0, 8 * GROUP)], ssend.at[w])
    wait_bytes(fr, fsend)
    wait_bytes(sr, tsend)
    wait_bytes(gr1, gsend.at[0])
    wait_bytes(gr2, gsend.at[1])
    wait_bytes(gr3, gsend.at[2])
    wait_bytes(gr3, gsend.at[3])
    wait_bytes(gr2, gsend.at[4])
    wait_bytes(gr1, gsend.at[5])
    wait_bytes(seven, nsend)
    wait_bytes(seven, osend)
    wait_bytes(outc, osem)
    wait_bytes(seven, orecv)


def on_device(uf, us, gf, gs, gain, upw, dnw, ad, au):
    any_spec = pl.BlockSpec(memory_space=pl.ANY)
    vmem = pl.BlockSpec(memory_space=pltpu.VMEM)
    sds = jax.ShapeDtypeStruct
    gain3 = gain.astype(F32).reshape(CHUNKS, 1, GROUP)
    dma = pltpu.SemaphoreType.DMA
    chunked = pltpu.VMEM((CHUNKS, T, GROUP), BF16)
    outs = pl.pallas_call(
        kernel,
        out_shape=(
            sds((T, 512), BF16), sds((T, 512), BF16), sds((T, 512), BF16), sds((T, D), BF16),
            sds((R, 512), F32), sds((R, 512), F32),
        ),
        in_specs=[any_spec] * 4 + [vmem] + [any_spec] * 4,
        out_specs=(vmem, vmem, vmem, any_spec, vmem, vmem),
        scratch_shapes=[
            chunked, chunked, chunked, chunked, chunked,
            pltpu.VMEM((CHUNKS, R, GROUP), BF16), pltpu.VMEM((CHUNKS, R, GROUP), BF16),
            pltpu.VMEM((D, H), BF16), pltpu.VMEM((D, H), BF16),
            pltpu.VMEM((T, H), F32), pltpu.VMEM((T, H), F32), pltpu.VMEM((T, H), F32),
            pltpu.VMEM((T, H), BF16), pltpu.VMEM((T, H), BF16),
            chunked, pltpu.VMEM((NM - 1, 2, T, GROUP), BF16),
            pltpu.VMEM((NZ, T, LAYER), BF16), pltpu.VMEM((NZ, NM - 1, SHARE, LAYER), BF16),
            pltpu.VMEM((NZ, SHARE, LAYER), BF16),
            pltpu.VMEM((T, R), F32), pltpu.VMEM((T, R), F32), pltpu.VMEM((T, 128), F32),
            pltpu.VMEM((T, 128), F32), pltpu.VMEM((SHARE, 128), F32), pltpu.VMEM((T, 128), F32),
            pltpu.VMEM((NM - 1, SHARE, 128), F32),
            pltpu.VMEM((2, 2, 8, 8, 256), F32), pltpu.VMEM((2, 8, 8, 256), F32),
            pltpu.VMEM((8, 8, 256), F32), pltpu.VMEM((7, 8, 256), F32),
            pltpu.VMEM((2, 2, 8, 8, 256), F32),
            dma((4,)), dma, dma((2, 4)), dma((2, 2)), dma((2, 8, 3)), dma((2,)), dma((2, 8)), dma((2,)),
            dma((2, 8)), dma((2,)),
            dma, dma, dma, dma((8,)), dma, dma, dma((6,)), dma((6,)), dma, dma, dma,
        ],
        compiler_params=pltpu.CompilerParams(
            collective_id=0, has_side_effects=True, vmem_limit_bytes=67000000
        ),
        name="coupling",
    )(uf, us, gf, gs, gain3, upw, dnw, ad.T, au)
    lf, ls, igf, igs, dgt, ug = outs
    return lf, ls, igf, igs, dgt.T, ug


def solution(mesh):
    return jax.shard_map(
        on_device,
        mesh=mesh,
        in_specs=(
            P("dp", None), P("dp", None), P("dp", None), P("dp", None), P(),
            P("dp", "mp"), P("dp", "mp"), P(), P(),
        ),
        out_specs=(
            P("dp", "mp"), P("dp", "mp"), P("dp", "mp"), P("dp", None), P("mp", None), P(None, "mp"),
        ),
        check_vma=False,
    )
```

time: 619 us -> 226 us (0.37)
  the two profiles are of different devices: /device:TPU:1 before, /device:TPU:45 now
where the time goes in v1:
time: 226 us
  Pallas kernels  214 us (95%)
  local copies, waits for them, and re-layouts  9.5 us (4%)
    pallas_call x1, Pallas kernels, on_device(): pl.pallas_call(kernel, out_shape=(sds((T, 512), BF16), sds((T, 512), BF16...  214 us
    unnamed x10, local copies, waits for them, and re-layouts  9.5 us

profile of v1, /device:TPU:45, one launch (start us, length us, event | category | flops | bytes accessed | tf_op | source)
XLA Modules:
  0.0 225.9 jit_solution(13104301592654184324)
XLA Ops:
  0.6 1.3 reshape.19
  1.9 214.5 %coupling.1 = (bf16[256,512]{1,0:T(8,128)(2,1)}, bf16[256,512]{1,0:T(8,128)(2,1)}, bf16[256,512]{1,0:T(8,128)(2,1)}, bf16[256,4096]{1,0:T(8,128)(2,1)}, f32[64,512]{1,0:T(8,128)}, /*index=5*/f32[64,512]{1,0:T(8,128)}) custom-call(bf16[256,4096]{1,0:T(8,128)(2,1)} %uf_hbm.1, bf16[256,4096]{1,0:T(8,128)(2,1)} %us_hbm.1, bf16[256,4096]{1,0:T(8,128)(2,1)} %gf_hbm.1, ...), custom_call_target="tpu_custom_call" | custom-call | tf_op jit(solution)/shard_map/coupling/pallas_call | solution.py:468
  216.4 1.7 copy.21
  218.1 1.7 copy.22
  219.8 1.7 copy.23
  221.4 0.0 copy-start.1
  221.4 0.0 copy-start
  221.4 3.2 %copy.24 = bf16[256,4096]{1,0:T(8,128)(2,1)} copy(bf16[256,4096]{1,0:T(8,128)(2,1)} %get-tuple-element.27) | data formatting | bytes 4194304
  224.6 0.0 copy-done.1
  224.6 0.7 copy.25
  225.3 0.0 copy-done
  225.3 0.7 copy.26
Async XLA Ops:
  221.4 3.2 %copy-start.1 = (f32[64,512]{1,0:T(8,128)S(1)}, f32[64,512]{1,0:T(8,128)}, u32[]{:S(2)}) copy-start(f32[64,512]{1,0:T(8,128)} %get-tuple-element.16) | copy-start | bytes 393220
  221.4 3.8 %copy-start = (f32[64,512]{1,0:T(8,128)S(1)}, f32[64,512]{1,0:T(8,128)}, u32[]{:S(2)}) copy-start(f32[64,512]{1,0:T(8,128)} %get-tuple-element.29) | copy-start | bytes 393220

commit v2 on v1

--- a/solution.py
+++ b/solution.py
@@ -48,18 +48,19 @@
     o_lf, o_ls, o_igf, o_igs, o_dg, o_ug,
     uf, us, gf, gs, norm, adt, au,
     up, dn, hp, ag, slope, act, pg,
-    fs, fr, ns, nr, outc,
+    fs, fr, f2s, fr2, ns, nr, outc,
     pre, sl, ssq, invb, curv, stat, sr,
     grad, gr1, gr2, gr3, gfin,
-    in_sem, ad_sem, init_sem, isend, zrecv, zsend, yrecv, ysend, srecv, ssend,
-    fsend, frecv, nsend, nrecv, tsend, trecv, gsend, grecv, osend, orecv, osem,
+    in_sem, ad_sem, yfirst, lsem, zrecv, zsend, yrecv, ysend, srecv, ssend,
+    fsend, frecv, f2sem, nsend, nrecv, tsend, trecv, gsend, grecv, osend, orecv, osem,
 ):
     dp = lax.axis_index("dp")
     m = lax.axis_index("mp")
     c = lax.rem(dp, 2)
     y = lax.rem(dp // 2, 2)
     z = dp // 4
-    home = jnp.where(y == c, 1, 0)
+    x = lax.rem(m, 4)
+    row_m = m - x
 
     def dev(z_, y_, c_, m_):
         return ((z_ * 2 + y_) * 2 + c_, m_)
@@ -86,28 +87,42 @@
     pl.semaphore_wait(barrier, len(partners))
 
     weights = ((upw, up), (dnw, dn))
-    first = z * LAYER + y * GROUP + c * 128
-    for w, (src, dst) in enumerate(weights):
-        for h in range(2):
-            rows = pl.ds(pl.multiple_of(first + h * UNIT, UNIT), UNIT)
-            piece = src.at[pl.ds(h * UNIT, UNIT)]
-            send(piece, dst.at[rows], isend.at[w, 0], init_sem.at[w, 2 * c + h], dev(z, 1 - y, y, m))
-
-            @pl.when(home == 1)
-            def _():
-                pltpu.make_async_copy(piece, dst.at[rows], init_sem.at[w, 2 * c + h]).start()
-
-            @pl.when(home == 0)
-            def _():
-                send(piece, dst.at[rows], isend.at[w, 1], init_sem.at[w, 2 * c + h], sib)
+    mine_row = z * LAYER + c * GROUP + y * 128
+
+    def first_y(w):
+        src, buf = weights[w]
+        for h, sem in ((0, yfirst.at[w]), (1, yrecv.at[w, 0])):
+            dst = buf.at[pl.ds(pl.multiple_of(mine_row + h * UNIT, UNIT), UNIT)]
+            send(src.at[pl.ds(h * UNIT, UNIT)], dst, ysend.at[w], sem, ypal)
+
+    def first_z(w):
+        src, buf = weights[w]
+        for j, h in ((0, 1), (1, 0)):
+            dst = buf.at[pl.ds(pl.multiple_of(mine_row + h * UNIT, UNIT), UNIT)]
+            send(src.at[pl.ds(h * UNIT, UNIT)], dst, zsend.at[w], zrecv.at[w, 1, j], znext)
+        dst = buf.at[pl.ds(pl.multiple_of(mine_row, 128), 128)]
+        send(src, dst, ssend.at[w], srecv.at[w, 0, 0], sib)
+        pltpu.make_async_copy(src, dst, lsem.at[w]).start()
+
+    first_y(0)
+    first_z(0)
+
+    def load_chunks(src, dst, sem):
+        def body(k, _):
+            col = pl.multiple_of((k // 2) * LAYER + lax.rem(k, 2) * 128, 128)
+            for yy in range(2):
+                pltpu.make_async_copy(
+                    src.at[:, pl.ds(col + yy * 256, 128)], dst.at[k, :, pl.ds(yy * 128, 128)], sem
+                ).start()
+            return 0
+
+        lax.fori_loop(0, CHUNKS, body, 0)
 
     ins = ((uf_hbm, uf), (gs_hbm, gs), (us_hbm, us), (gf_hbm, gf))
     for src, dst in ((adt_hbm, adt), (au_hbm, au)):
-        for k in range(CHUNKS):
-            pltpu.make_async_copy(src.at[:, pl.ds(k * GROUP, GROUP)], dst.at[k], ad_sem).start()
+        load_chunks(src, dst, ad_sem)
     for i, (src, dst) in enumerate(ins):
-        for k in range(CHUNKS):
-            pltpu.make_async_copy(src.at[:, pl.ds(k * GROUP, GROUP)], dst.at[k], in_sem.at[i]).start()
+        load_chunks(src, dst, in_sem.at[i])
 
     def own_layer(s):
         return lax.rem(jnp.where(c == 0, z + NZ - s, z + s), NZ)
@@ -122,29 +137,32 @@
         first_step = isinstance(s, int) and s == 0
         buf = weights[w][1]
         layer = own_layer(s)
-        for j in range(CARRY):
-            region = buf.at[rows_at(layer, c, UNIT * home + UNIT * j, UNIT)]
-            wait_bytes(region, init_sem.at[w, j + home] if first_step else zrecv.at[w, s, j])
+        for j, offset in enumerate((y * 128 + UNIT, y * 128, (1 - y) * 128)):
+            if first_step and j < 2:
+                continue
+            region = buf.at[rows_at(layer, c, offset, UNIT)]
+            wait_bytes(region, yfirst.at[w] if first_step else zrecv.at[w, s, j])
 
             @pl.when(s < NZ - 1)
             def _():
                 send(region, region, zsend.at[w], zrecv.at[w, s + 1, j], znext)
 
-        if not first_step:
-            region = buf.at[rows_at(layer, c, 3 * UNIT * home, UNIT)]
-            send(region, region, ysend.at[w], yrecv.at[w, s], ypal)
+            if j == 0:
+                send(region, region, ysend.at[w], yrecv.at[w, s], ypal)
+            if j == 1:
+                both = buf.at[rows_at(layer, c, y * 128, 128)]
+                send(both, both, ssend.at[w], srecv.at[w, s, 0], sib)
 
     def late(w, s):
-        first_step = isinstance(s, int) and s == 0
         buf = weights[w][1]
         layer = own_layer(s)
-        region = buf.at[rows_at(layer, c, 3 * UNIT * (1 - home), UNIT)]
-        wait_bytes(region, init_sem.at[w, 3 * (1 - home)] if first_step else yrecv.at[w, s])
-        region = buf.at[rows_at(layer, c, 0, GROUP)]
-        send(region, region, ssend.at[w], srecv.at[w, s], sib)
+        wait_bytes(buf.at[rows_at(layer, c, (1 - y) * 128 + UNIT, UNIT)], yrecv.at[w, s])
+        region = buf.at[rows_at(layer, c, (1 - y) * 128, 128)]
+        send(region, region, ssend.at[w], srecv.at[w, s, 1], sib)
 
     def ready(w, s):
-        wait_bytes(weights[w][1].at[rows_at(sib_layer(s), 1 - c, 0, GROUP)], srecv.at[w, s])
+        for i, yy in ((0, y), (1, 1 - y)):
+            wait_bytes(weights[w][1].at[rows_at(sib_layer(s), 1 - c, yy * 128, 128)], srecv.at[w, s, i])
 
     def product_step(w, s, left, acc):
         buf = weights[w][1]
@@ -161,11 +179,12 @@
     def frozen_block(layer, group):
         k = layer * 2 + group
         fs[k] = dot_nt(act[...], dn[rows_at(layer, group, 0, GROUP), :]).astype(BF16)
-        shift = lax.rem(layer + NM - m, NM)
+        to_x = lax.rem(layer, 4)
+        shift = lax.rem(to_x + 4 - x, 4)
 
         @pl.when(shift != 0)
         def _():
-            send(fs.at[k], fr.at[shift - 1, group], fsend, frecv, (dp, layer))
+            send(fs.at[k], fr.at[shift - 1, layer // 4, group], fsend, frecv, (dp, row_m + to_x))
 
     def down_step(s):
         ready(1, s)
@@ -271,7 +290,9 @@
                 for t in range(4):
                     for q in range(2):
                         lo = yy * 32 + t * 8
-                        out[lo:lo + 8, q * 256:q * 256 + 256] = gfin[half, yy, 2 * t + q]
+                        piece = gfin[half, yy, 2 * t + q]
+                        out[lo:lo + 8, q * 128:q * 128 + 128] = piece[:, :128]
+                        out[lo:lo + 8, q * 128 + 256:q * 128 + 384] = piece[:, 128:]
 
     def activations():
         def body(i, _):
@@ -286,9 +307,10 @@
 
     def slices_out():
         for q in range(2):
-            lo = q * 256
-            o_ls[:, lo:lo + 256] = us[2 * m + q]
-            o_igf[:, lo:lo + 256] = (0.5 * gf[2 * m + q].astype(F32)).astype(BF16)
+            for yy in range(2):
+                lo, src = q * 128 + yy * 256, slice(yy * 128, yy * 128 + 128)
+                o_ls[:, lo:lo + 128] = us[2 * m + q, :, src]
+                o_igf[:, lo:lo + 128] = (0.5 * gf[2 * m + q, :, src].astype(F32)).astype(BF16)
 
     poll(0, 0)
     adapter_in()
@@ -307,6 +329,7 @@
 
         @pl.when(s == 4)
         def _():
+            first_y(1)
             grads_1()
 
         @pl.when(s == 5)
@@ -315,6 +338,7 @@
 
         @pl.when(s == 6)
         def _():
+            first_z(1)
             grads_3()
 
         hidden_step(s - 3)
@@ -322,6 +346,7 @@
 
     late_done = 3
     poll(0, 3)
+    wait_bytes(up.at[pl.ds(0, 128)], lsem.at[0])
     hidden_step(0)
     lax.fori_loop(late_done + 1, NZ, up_body, 0)
     poll(1, 0)
@@ -330,6 +355,7 @@
     hidden_step(6)
     late(1, 0)
     poll(1, 1)
+    wait_bytes(dn.at[pl.ds(0, 128)], lsem.at[1])
     hidden_step(7)
     activations()
 
@@ -388,18 +414,22 @@
     lax.fori_loop(0, NZ, normed_block, 0)
 
     wait_bytes(fr, frecv)
+    far = 4 - row_m + x
+
+    def row_sum(q, half, layer, rows):
+        total = fs[2 * layer + q, rows, :].astype(F32)
+        for k in range(3):
+            total = total + fr[k, half, q, rows, :].astype(F32)
+        return total
+
     for q in range(2):
-        def rebuild(i, _):
+        def far_half(i, _):
             rows = pl.ds(pl.multiple_of(i * 32, 32), 32)
-            total = fs[2 * m + q, rows, :].astype(F32)
-            for k in range(NM - 1):
-                total = total + fr[k, q, rows, :].astype(F32)
-            o_lf[rows, q * GROUP:q * GROUP + GROUP] = (
-                (uf[2 * m + q, rows, :].astype(F32) - total) * 2.0
-            ).astype(BF16)
-            return 0
-
-        lax.fori_loop(0, 8, rebuild, 0)
+            f2s[q, rows, :] = row_sum(q, far // 4, far, rows).astype(BF16)
+            return 0
+
+        lax.fori_loop(0, 8, far_half, 0)
+    send(f2s, fr2, f2sem.at[0], f2sem.at[1], (dp, far))
 
     wait_bytes(sr, trecv)
     inv32 = invb[mine, :]
@@ -419,11 +449,13 @@
             normed_grad = ns[b, mine, lo:lo + GROUP].astype(F32)
             for k in range(NM - 1):
                 normed_grad = normed_grad + nr[b, k, :, lo:lo + GROUP].astype(F32)
-            outc[b, :, lo:lo + GROUP] = (
+            value = (
                 gs[k2, mine, :].astype(F32)
                 + inv * gain_ref[k2] * normed_grad
                 - us[k2, mine, :].astype(F32) * cv
             ).astype(BF16)
+            outc[b, :, q * 128:q * 128 + 128] = value[:, :128]
+            outc[b, :, q * 128 + 256:q * 128 + 384] = value[:, 128:]
         place = o_igs.at[mine, pl.ds(pl.multiple_of(b * LAYER, LAYER), LAYER)]
         for k in range(1, NM):
             send(outc.at[b], place, osend, orecv, mdev[k])
@@ -432,19 +464,27 @@
 
     lax.fori_loop(0, NZ, finish, 0)
 
+    wait_bytes(fr2, f2sem.at[1])
+    for q in range(2):
+        def rebuild(i, _):
+            rows = pl.ds(pl.multiple_of(i * 32, 32), 32)
+            total = row_sum(q, m // 4, m, rows) + fr2[q, rows, :].astype(F32)
+            value = ((uf[2 * m + q, rows, :].astype(F32) - total) * 2.0).astype(BF16)
+            for yy in range(2):
+                lo = q * 128 + yy * 256
+                o_lf[rows, lo:lo + 128] = value[:, yy * 128:yy * 128 + 128]
+            return 0
+
+        lax.fori_loop(0, 8, rebuild, 0)
+
     seven = ns.at[:, pl.ds(0, T - SHARE)]
     for w in range(2):
         buf = weights[w][1]
-        wait_bytes(buf.at[pl.ds(0, 2 * UNIT)], isend.at[w, 0])
-
-        @pl.when(home == 0)
-        def _():
-            wait_bytes(buf.at[pl.ds(0, 2 * UNIT)], isend.at[w, 1])
-
         wait_bytes(buf.at[pl.ds(0, 7 * CARRY * UNIT)], zsend.at[w])
-        wait_bytes(buf.at[pl.ds(0, 7 * UNIT)], ysend.at[w])
+        wait_bytes(buf.at[pl.ds(0, 9 * UNIT)], ysend.at[w])
         wait_bytes(buf.at[pl.ds(0, 8 * GROUP)], ssend.at[w])
     wait_bytes(fr, fsend)
+    wait_bytes(f2s, f2sem.at[0])
     wait_bytes(sr, tsend)
     wait_bytes(gr1, gsend.at[0])
     wait_bytes(gr2, gsend.at[1])
@@ -458,11 +498,23 @@
     wait_bytes(seven, orecv)
 
 
+def publish(*refs):
+    ins, outs, bufs, sem = refs[:6], refs[6:12], refs[12:18], refs[18]
+    order = (3, 0, 1, 2, 4, 5)
+    for i in order:
+        pltpu.make_async_copy(ins[i], bufs[i], sem.at[i, 0]).start()
+    for i in order:
+        pltpu.make_async_copy(ins[i], bufs[i], sem.at[i, 0]).wait()
+        pltpu.make_async_copy(bufs[i], outs[i], sem.at[i, 1]).start()
+    for i in order:
+        pltpu.make_async_copy(bufs[i], outs[i], sem.at[i, 1]).wait()
+
+
 def on_device(uf, us, gf, gs, gain, upw, dnw, ad, au):
     any_spec = pl.BlockSpec(memory_space=pl.ANY)
     vmem = pl.BlockSpec(memory_space=pltpu.VMEM)
     sds = jax.ShapeDtypeStruct
-    gain3 = gain.astype(F32).reshape(CHUNKS, 1, GROUP)
+    gain3 = gain.astype(F32).reshape(NZ, 2, 2, 128).swapaxes(1, 2).reshape(CHUNKS, 1, GROUP)
     dma = pltpu.SemaphoreType.DMA
     chunked = pltpu.VMEM((CHUNKS, T, GROUP), BF16)
     outs = pl.pallas_call(
@@ -479,7 +531,8 @@
             pltpu.VMEM((D, H), BF16), pltpu.VMEM((D, H), BF16),
             pltpu.VMEM((T, H), F32), pltpu.VMEM((T, H), F32), pltpu.VMEM((T, H), F32),
             pltpu.VMEM((T, H), BF16), pltpu.VMEM((T, H), BF16),
-            chunked, pltpu.VMEM((NM - 1, 2, T, GROUP), BF16),
+            chunked, pltpu.VMEM((3, 2, 2, T, GROUP), BF16),
+            pltpu.VMEM((2, T, GROUP), BF16), pltpu.VMEM((2, T, GROUP), BF16),
             pltpu.VMEM((NZ, T, LAYER), BF16), pltpu.VMEM((NZ, NM - 1, SHARE, LAYER), BF16),
             pltpu.VMEM((NZ, SHARE, LAYER), BF16),
             pltpu.VMEM((T, R), F32), pltpu.VMEM((T, R), F32), pltpu.VMEM((T, 128), F32),
@@ -488,16 +541,23 @@
             pltpu.VMEM((2, 2, 8, 8, 256), F32), pltpu.VMEM((2, 8, 8, 256), F32),
             pltpu.VMEM((8, 8, 256), F32), pltpu.VMEM((7, 8, 256), F32),
             pltpu.VMEM((2, 2, 8, 8, 256), F32),
-            dma((4,)), dma, dma((2, 4)), dma((2, 2)), dma((2, 8, 3)), dma((2,)), dma((2, 8)), dma((2,)),
-            dma((2, 8)), dma((2,)),
-            dma, dma, dma, dma((8,)), dma, dma, dma((6,)), dma((6,)), dma, dma, dma,
+            dma((4,)), dma, dma((2,)), dma((2,)), dma((2, 8, 3)), dma((2,)), dma((2, 8)), dma((2,)),
+            dma((2, 8, 2)), dma((2,)),
+            dma, dma, dma((2,)), dma, dma((8,)), dma, dma, dma((6,)), dma((6,)), dma, dma, dma,
         ],
         compiler_params=pltpu.CompilerParams(
             collective_id=0, has_side_effects=True, vmem_limit_bytes=67000000
         ),
         name="coupling",
     )(uf, us, gf, gs, gain3, upw, dnw, ad.T, au)
-    lf, ls, igf, igs, dgt, ug = outs
+    lf, ls, igf, igs, dgt, ug = pl.pallas_call(
+        publish,
+        out_shape=tuple(sds(o.shape, o.dtype) for o in outs),
+        in_specs=[any_spec] * 6,
+        out_specs=(any_spec,) * 6,
+        scratch_shapes=[pltpu.VMEM(o.shape, o.dtype) for o in outs] + [dma((6, 2))],
+        name="publish",
+    )(*outs)
     return lf, ls, igf, igs, dgt.T, ug
 
 

time: 226 us -> 171 us (0.76)
  the two profiles are of different devices: /device:TPU:45 before, /device:TPU:1 now
where the time goes in v2:
time: 171 us
  Pallas kernels  169 us (99%)
    pallas_call x1, Pallas kernels, on_device(): pl.pallas_call(kernel, out_shape=(sds((T, 512), BF16), sds((T, 512), BF16...  166 us

profile of v2, /device:TPU:1, one launch (start us, length us, event | category | flops | bytes accessed | tf_op | source)
XLA Modules:
  0.0 171.0 jit_solution(1599640549153697238)
XLA Ops:
  0.6 0.7 convert_bitcast_fusion
  1.3 0.6 copy.15
  2.0 165.7 %coupling.1 = (bf16[256,512]{1,0:T(8,128)(2,1)}, bf16[256,512]{1,0:T(8,128)(2,1)}, bf16[256,512]{1,0:T(8,128)(2,1)}, bf16[256,4096]{1,0:T(8,128)(2,1)}, f32[64,512]{1,0:T(8,128)}, /*index=5*/f32[64,512]{1,0:T(8,128)}) custom-call(bf16[256,4096]{1,0:T(8,128)(2,1)} %uf_hbm.1, bf16[256,4096]{1,0:T(8,128)(2,1)} %us_hbm.1, bf16[256,4096]{1,0:T(8,128)(2,1)} %gf_hbm.1, ...), custom_call_target="tpu_custom_call" | custom-call | tf_op jit(solution)/shard_map/coupling/pallas_call | solution.py:520
  167.7 3.3 %publish.1 = (bf16[256,512]{1,0:T(8,128)(2,1)}, bf16[256,512]{1,0:T(8,128)(2,1)}, bf16[256,512]{1,0:T(8,128)(2,1)}, bf16[256,4096]{1,0:T(8,128)(2,1)}, f32[64,512]{1,0:T(8,128)}, /*index=5*/f32[64,512]{1,0:T(8,128)}) custom-call(bf16[256,512]{1,0:T(8,128)(2,1)} %get-tuple-element.18.refs_0_, bf16[256,512]{1,0:T(8,128)(2,1)} %get-tuple-element.19.refs_1_, ...), custom_call_target="tpu_custom_call" | custom-call | tf_op jit(solution)/shard_map/publish/pallas_call | solution.py:553
